TPU v7x, 512 devices: a whole 4x8x8 slice. The times are simulated.
512 devices in a mesh: dp: 4 (over x), ep: 128 (over z, y, core).
Axes of the slice: x: 4, y: 8, z: 8, core: 2. Of those that a mesh axis runs over, the one named last changes fastest.
Arguments:
- tokens: bfloat16 [128, 16, 2048], P('ep', 'dp'), may hold values from -6 to 6
- dest_ids: int32 [128, 16, 8], P('ep', 'dp'), may hold values from 0 to 127, all different within a row; in each aligned block of 16 rows (0 to 15, 16 to 31, ..., all dimensions but the last counted through in order) at most 2 rows name the same one
- gate_fixed: int32 [128, 16, 8], P('ep', 'dp'), may hold values from 1 to 65535
- gate_up: bfloat16 [128, 2, 768, 2048], P('ep', None, 'dp'), may hold values from -0.125 to 0.125
- down: bfloat16 [128, 768, 2048], P('ep', 'dp'), may hold values from -0.21875 to 0.21875
Outputs:
- mixed: bfloat16 [128, 16, 2048], P('ep', 'dp')
Inputs may be any that keep to these rules, and one draw needn't show every extreme that they name: `dest_ids`: each row names 8 different experts; within one column's 16 rows no expert is named by more than 2 routes.
All inputs are finite; a program needn't handle non-finite values.
Results may differ from a plain program's by a relative error of at most 0.012.
Values may be sent and summed in bfloat16 or wider, within the bound.
A program may use at most 192 MiB of HBM per device.

v0:
```python
import jax
import jax.numpy as jnp
from jax import lax
from jax.sharding import PartitionSpec as P


def feed_forward(rows, pair, lower):
    gate = jnp.einsum("nd,hd->nh", rows, pair[0], preferred_element_type=jnp.float32)
    upper = jnp.einsum("nd,hd->nh", rows, pair[1], preferred_element_type=jnp.float32)
    hidden = (jax.nn.silu(gate) * upper).astype(jnp.bfloat16)
    return jnp.dot(hidden, lower, preferred_element_type=jnp.float32).astype(jnp.bfloat16)


def per_device(tokens, dest_ids, gate_fixed, gate_up, down):
    peer_count = lax.axis_size("ep")
    own_rows = tokens[0]
    width = own_rows.shape[1]
    top_count = dest_ids.shape[2]
    route_table = jnp.concatenate([dest_ids[0], gate_fixed[0]], axis=1)
    column_table = lax.all_gather(route_table, "dp", axis=0, tiled=True)
    col_rows = column_table.shape[0]
    capacity = min(col_rows, max(2, 2 * col_rows * top_count // peer_count))
    target_dev = column_table[:, :top_count].reshape(-1)
    gate_raw = column_table[:, top_count:].astype(jnp.float32)
    gate_norm = gate_raw / jnp.sum(gate_raw, axis=1, keepdims=True)
    marks = (target_dev[:, None] == jnp.arange(peer_count, dtype=jnp.int32)[None, :]).astype(
        jnp.int32
    )
    slot_rank = jnp.sum(jnp.cumsum(marks, axis=0) * marks, axis=1) - 1
    slot_index = target_dev * capacity + slot_rank
    source_row = jnp.arange(target_dev.shape[0], dtype=jnp.int32) // top_count
    column_rows = lax.all_gather(own_rows, "dp", axis=0, tiled=True)
    send_block = (
        jnp.zeros((peer_count * capacity, width), jnp.bfloat16)
        .at[slot_index]
        .set(column_rows[source_row])
        .reshape(peer_count, capacity, width)
    )
    rows = lax.all_to_all(send_block, "ep", split_axis=0, concat_axis=0, tiled=True)
    flat_rows = rows.reshape(-1, rows.shape[2])
    own_out = feed_forward(flat_rows, gate_up[0], down[0])
    returned = lax.all_to_all(
        own_out.reshape(rows.shape[0], rows.shape[1], -1),
        "ep",
        split_axis=0,
        concat_axis=0,
        tiled=True,
    )
    flat_back = returned.reshape(peer_count * capacity, -1)
    weighted = flat_back[slot_index].astype(jnp.float32) * gate_norm.reshape(-1)[:, None]
    summed = jnp.sum(weighted.reshape(col_rows, top_count, -1), axis=1)
    mine = lax.psum_scatter(summed.astype(jnp.bfloat16), "dp", scatter_dimension=0, tiled=True)
    return mine[None]


def solution(mesh):
    return jax.shard_map(
        per_device,
        mesh=mesh,
        in_specs=(
            P("ep", "dp", None),
            P("ep", "dp", None),
            P("ep", "dp", None),
            P("ep", None, "dp", None),
            P("ep", "dp", None),
        ),
        out_specs=P("ep", "dp", None),
        check_vma=False,
    )
```

profile of v0, /device:TPU:8, one launch (start us, length us, event | category | flops | bytes accessed | tf_op | source)
XLA Modules:
  0.0 182.8 jit_solution(7191116500669155721)
XLA Ops:
  6.5 0.0 copy-start
  6.5 0.8 add_bitcast_fusion
  7.4 11.1 %all-gather.1 = s32[4,4,16]{2,1,0:T(4,128)S(1)} all-gather(s32[1,4,16]{2,1,0:T(4,128)S(1)} %add_bitcast_fusion), channel_id=1, replica_groups=mesh['dp'=4,'ep'=128] {'dp'}, dimensions={0}, use_global_device_ids=true | all-gather | bytes 1280 | tf_op jit(solution)/shard_map/all_gather | solution.py:20
  18.5 0.1 eq.15
  18.6 0.1 fusion.19
  18.7 0.2 reduce_window_sum.11
  18.9 0.2 select_reduce_fusion
  19.1 0.1 mul.37
  19.2 0.7 copy.7
  19.9 12.0 %all-gather = bf16[1,16,2048]{2,0,1:T(2,128)(2,1)S(1)} all-gather(bf16[1,4,2048]{2,0,1:T(2,128)(2,1)S(1)} %copy.7), channel_id=2, replica_groups=mesh['dp'=4,'ep'=128] {'dp'}, dimensions={1}, use_global_device_ids=true | all-gather | bytes 81920 | tf_op jit(solution)/shard_map/all_gather | solution.py:32
  32.0 3.4 %scatter_custom_fusion = bf16[256,2048]{1,0:T(8,128)(2,1)S(1)} fusion(s32[128]{0:T(128)S(1)} %fusion.23, bf16[16,2048]{1,0:T(8,128)(2,1)S(1)} %bitcast.37, s32[1024]{0:T(1024)S(1)} %pad_clamp_fusion.1, bf16[]{:T(256)} %constant.28.clone.1), kind=kCustom, calls=%fused_computation.14 | custom fusion | bytes 1048578 | tf_op jit(solution)/shard_map/scatter | solution.py:36
  35.4 0.7 reshape.105
  36.1 48.6 %all_to_all.10 = bf16[128,2,2048]{2,1,0:T(2,128)(2,1)S(1)} all-to-all(bf16[128,2,2048]{2,1,0:T(2,128)(2,1)S(1)} %reshape.105), channel_id=1, replica_groups=mesh['dp'=4,'ep'=128] {'ep'}, dimensions={0} | all-to-all | bytes 2097152 | tf_op jit(solution)/shard_map/all_to_all | solution.py:39
  84.7 0.4 reshape.106
  85.1 1.6 fusion.5
  86.8 0.0 copy-done
  86.8 2.6 %convolution_convert_fusion = bf16[256,2048]{1,0:T(8,128)(2,1)S(1)} fusion(bf16[256,2048]{1,0:T(8,128)(2,1)S(1)} %reshape.106, bf16[1,192,2048]{2,1,0:T(8,128)(2,1)S(1)} %copy-done, bf16[1,2,192,2048]{3,2,1,0:T(8,128)(2,1)} %param.8, f32[256,192]{0,1:T(8,128)S(1)} %fusion.5), kind=kOutput, calls=%fused_computation.3 | convolution fusion | flops 403472384 | bytes 3866624 | tf_op jit(solution)/shard_map/dot_general | solution.py:11
  89.3 1.5 reshape.107
  90.9 5.9 %all-to-all-start.1 = ((bf16[128,2,2048]{2,1,0:T(2,128)(2,1)}), bf16[128,2,2048]{2,1,0:T(2,128)(2,1)S(1)}, u32[]{:S(2)}, u32[]{:S(2)}) async-start(bf16[128,2,2048]{2,1,0:T(2,128)(2,1)} %reshape.107), calls=%async_computation.1 | async-start | bytes 2097152 | tf_op jit(solution)/shard_map/all_to_all | solution.py:42
  96.8 0.0 all-reduce.3.cloned.1.call-start
  96.9 0.2 fusion.21
  97.0 0.1 fusion.20
  97.1 31.1 %all-to-all-done.1 = bf16[128,2,2048]{2,1,0:T(2,128)(2,1)S(1)} async-done(((bf16[128,2,2048]{2,1,0:T(2,128)(2,1)}), bf16[128,2,2048]{2,1,0:T(2,128)(2,1)S(1)}, u32[]{:S(2)}, u32[]{:S(2)}) %all-to-all-start.1) | async-done | bytes 1048608 | tf_op jit(solution)/shard_map/all_to_all | solution.py:42
  128.2 0.4 reshape.108
  128.7 0.9 gather_fusion
  129.6 1.1 fusion.1
  130.7 0.0 all-reduce.3.cloned.1.call-update
  130.7 1.3 dynamic-slice
  132.6 42.0 %all-reduce.3.cloned.1.call-done = bf16[16,2048]{1,0:T(8,128)(2,1)} async-done(((bf16[16,2048]{1,0:T(8,128)(2,1)}), bf16[16,2048]{1,0:T(8,128)(2,1)}) %all-reduce.3.cloned.1.call-update) | async-done | bytes 65552
  174.6 1.4 dynamic-slice_bitcast_fusion
  (6 shorter events, 0.1 us)
Async XLA Ops:
  6.5 80.2 %copy-start = (bf16[1,192,2048]{2,1,0:T(8,128)(2,1)S(1)}, bf16[1,192,2048]{2,1,0:T(8,128)(2,1)}, u32[]{:S(2)}) copy-start(bf16[1,192,2048]{2,1,0:T(8,128)(2,1)} %param.9) | copy-start | bytes 2359300
  90.9 37.4 %all-to-all-start.1 = ((bf16[128,2,2048]{2,1,0:T(2,128)(2,1)}), bf16[128,2,2048]{2,1,0:T(2,128)(2,1)S(1)}, u32[]{:S(2)}, u32[]{:S(2)}) async-start(bf16[128,2,2048]{2,1,0:T(2,128)(2,1)} %reshape.107), calls=%async_computation.1 | async-start | bytes 2097152 | tf_op jit(solution)/shard_map/all_to_all | solution.py:42
  96.8 77.8 %all-reduce.3.cloned.1.call-start = ((), (), s32[]{:S(2)}) async-start(), calls=%async_computation.2 | async-start | bytes 131072
Sparse Core Ops, SparseCore 0:
  130.8 43.7 all-reduce.2
where the time goes:
time: 183 us
  waiting for transfers between devices  73.1 us (40%)
  blocking collectives  71.7 us (39%)
  between operations  14.2 us (8%)
  local copies, waits for them, and re-layouts  11 us (6%)
  starting transfers between devices  5.97 us (3%)
  matrix products  4.21 us (2%)
  other arithmetic  2.64 us (1%)
    all_to_all x1, blocking collectives, per_device(): lax.all_to_all(send_block, 'ep', split_axis=0, concat_axis=0, tiled=True)  48.6 us
    unnamed x2, waiting for transfers between devices  42 us
    all_to_all x1, waiting for transfers between devices, per_device(): lax.all_to_all(own_out.reshape(rows.shape[0], rows.shape[1], -1), 'ep', s...  31.1 us
    all_gather x1, blocking collectives, per_device(): column_rows = lax.all_gather(own_rows, 'dp', axis=0, tiled=True)  12 us
    all_gather x1, blocking collectives, per_device(): column_table = lax.all_gather(route_table, 'dp', axis=0, tiled=True)  11.1 us
    all_to_all x1, starting transfers between devices, per_device(): lax.all_to_all(own_out.reshape(rows.shape[0], rows.shape[1], -1), 'ep', s...  5.93 us
  transfers between devices with their start and end apart: 2, of which 2 were waited for; matrix products, arithmetic and copies ran while one was open for 1% of the time, Pallas kernels for 0%

commit v1 on v0

--- a/solution.py
+++ b/solution.py
@@ -2,6 +2,12 @@
 import jax.numpy as jnp
 from jax import lax
 from jax.sharding import PartitionSpec as P
+
+
+def laid_out(blocks, dim):
+    blocks = jnp.moveaxis(blocks, 0, dim)
+    dims = blocks.shape
+    return blocks.reshape(*dims[:dim], dims[dim] * dims[dim + 1], *dims[dim + 2 :])
 
 
 def feed_forward(rows, pair, lower):
@@ -29,7 +35,19 @@
     slot_rank = jnp.sum(jnp.cumsum(marks, axis=0) * marks, axis=1) - 1
     slot_index = target_dev * capacity + slot_rank
     source_row = jnp.arange(target_dev.shape[0], dtype=jnp.int32) // top_count
-    column_rows = lax.all_gather(own_rows, "dp", axis=0, tiled=True)
+    size = lax.axis_size("dp")
+    pairs = [(i, (i + 1) % size) for i in range(size)]
+    back = [(b, a) for a, b in pairs]
+    lower_2, upper_2 = ([], [])
+    for turn in range(size - 1):
+        if turn % 2 == 0:
+            lower_2.append(lax.ppermute(lower_2[-1] if lower_2 else own_rows, "dp", pairs))
+        else:
+            upper_2.append(lax.ppermute(upper_2[-1] if upper_2 else own_rows, "dp", back))
+    parts = jnp.stack([*lower_2[::-1], own_rows, *upper_2])
+    shift = lax.axis_index("dp") - len(lower_2)
+    parts = parts[(jnp.arange(size) - shift) % size]
+    column_rows = laid_out(parts, 0)
     send_block = (
         jnp.zeros((peer_count * capacity, width), jnp.bfloat16)
         .at[slot_index]

time: 183 us -> 185 us (1.011)
  blocking collectives: 71.7 us -> 59 us
  starting transfers between devices: 5.97 us -> 15.8 us
  waiting for transfers between devices: 73.1 us -> 76.7 us
    all_gather x1 -> x0, blocking collectives: 12 us -> none  [per_device(): column_rows = lax.all_gather(own_rows, 'dp', axis=0, tiled=True)]
    ppermute x0 -> x3, starting transfers between devices: none -> 9.79 us  [the longest x2 6.14 us: per_device(): lax.ppermute(lower_2[-1] if lower_2 else own_rows, 'dp', pairs)]
    ppermute x0 -> x3, waiting for transfers between devices: none -> 4.2 us  [the longest x2 4.2 us: per_device(): lax.ppermute(lower_2[-1] if lower_2 else own_rows, 'dp', pairs)]
  transfers between devices with their start and end apart: 2 -> 5, of which waited for: 2 -> 3; matrix products, arithmetic and copies ran while one was open for 1% -> 2% of each run, Pallas kernels for 0% -> 0%
where the time goes in v1:
time: 185 us; the launch traced here: 184 us
  waiting for transfers between devices  76.7 us (41%)
  blocking collectives  59 us (32%)
  starting transfers between devices  15.8 us (9%)
  between operations  14.2 us (8%)
  local copies, waits for them, and re-layouts  10.8 us (6%)
  matrix products  4.2 us (2%)
  other arithmetic  3.35 us (2%)
    all_to_all x1, blocking collectives, per_device(): lax.all_to_all(send_block, 'ep', split_axis=0, concat_axis=0, tiled=True)  48.6 us
    unnamed x2, waiting for transfers between devices  41.4 us
    all_to_all x1, waiting for transfers between devices, per_device(): lax.all_to_all(own_out.reshape(rows.shape[0], rows.shape[1], -1), 'ep', s...  31.1 us
    all_gather x1, blocking collectives, per_device(): column_table = lax.all_gather(route_table, 'dp', axis=0, tiled=True)  10.4 us
    ppermute x2, starting transfers between devices, per_device(): lax.ppermute(lower_2[-1] if lower_2 else own_rows, 'dp', pairs)  6.14 us
    all_to_all x1, starting transfers between devices, per_device(): lax.all_to_all(own_out.reshape(rows.shape[0], rows.shape[1], -1), 'ep', s...  5.93 us
    ppermute x2, waiting for transfers between devices, per_device(): lax.ppermute(lower_2[-1] if lower_2 else own_rows, 'dp', pairs)  4.2 us
  transfers between devices with their start and end apart: 5, of which 3 were waited for; matrix products, arithmetic and copies ran while one was open for 2% of the time, Pallas kernels for 0%

profile of v1, /device:TPU:8, one launch (start us, length us, event | category | flops | bytes accessed | tf_op | source)
XLA Modules:
  0.0 184.2 jit_solution(13150295631261179928)
XLA Ops:
  6.5 0.0 copy-start
  6.5 3.5 %collective-permute-start = (bf16[4,2048]{1,0:T(4,128)(2,1)}, bf16[4,2048]{1,0:T(4,128)(2,1)S(1)}, u32[]{:S(2)}, u32[]{:S(2)}) collective-permute-start(bf16[4,2048]{1,0:T(4,128)(2,1)} %bitcast.40), channel_id=1, source_target_pairs={{0,128},{128,256},{256,384},{384,0},{1,129},{129,257},{257,385},{3... | collective-permute-start | bytes 49160 | tf_op jit(solution)/shard_map/ppermute | solution.py:44
  10.1 3.7 %collective-permute-start.2 = (bf16[4,2048]{1,0:T(4,128)(2,1)}, bf16[4,2048]{1,0:T(4,128)(2,1)S(1)}, u32[]{:S(2)}, u32[]{:S(2)}) collective-permute-start(bf16[4,2048]{1,0:T(4,128)(2,1)} %bitcast.41), channel_id=1, source_target_pairs={{128,0},{256,128},{384,256},{0,384},{129,1},{257,129},{385,257},{1... | collective-permute-start | bytes 49160 | tf_op jit(solution)/shard_map/ppermute | solution.py:46
  13.7 0.8 add_bitcast_fusion
  14.5 10.4 %all-gather = s32[4,4,16]{2,1,0:T(4,128)S(1)} all-gather(s32[1,4,16]{2,1,0:T(4,128)S(1)} %add_bitcast_fusion), channel_id=1, replica_groups=mesh['dp'=4,'ep'=128] {'dp'}, dimensions={0}, use_global_device_ids=true | all-gather | bytes 1280 | tf_op jit(solution)/shard_map/all_gather | solution.py:26
  24.9 0.1 eq.17
  25.0 0.1 fusion.19
  25.1 0.2 reduce_window_sum.11
  25.3 0.2 select_reduce_fusion
  25.5 0.1 mul.37
  25.6 0.0 collective-permute-done
  25.6 2.6 %collective-permute-start.1 = (bf16[4,2048]{1,0:T(4,128)(2,1)S(1)}, bf16[4,2048]{1,0:T(4,128)(2,1)S(1)}, u32[]{:S(2)}, u32[]{:S(2)}) collective-permute-start(bf16[4,2048]{1,0:T(4,128)(2,1)S(1)} %collective-permute-done), channel_id=1, source_target_pairs={{0,128},{128,256},{256,384},{384,0},{1,129},{129,257},{257,385},{3... | collective-permute-start | bytes 49160 | tf_op jit(solution)/shard_map/ppermute | solution.py:44
  28.3 0.0 collective-permute-done.2
  28.3 4.2 %collective-permute-done.1 = bf16[4,2048]{1,0:T(4,128)(2,1)S(1)} collective-permute-done((bf16[4,2048]{1,0:T(4,128)(2,1)S(1)}, bf16[4,2048]{1,0:T(4,128)(2,1)S(1)}, u32[]{:S(2)}, u32[]{:S(2)}) %collective-permute-start.1) | collective-permute-done | bytes 16416 | tf_op jit(solution)/shard_map/ppermute | solution.py:44
  32.5 0.8 pad_maximum_fusion
  33.3 0.6 gather_fusion
  33.9 3.4 %scatter_custom_fusion = bf16[256,2048]{1,0:T(8,128)(2,1)S(1)} fusion(s32[128]{0:T(128)S(1)} %fusion.24, bf16[16,2048]{1,0:T(8,128)(2,1)S(1)} %reshape.157, s32[1024]{0:T(1024)S(1)} %pad_clamp_fusion.1, bf16[]{:T(256)} %constant.48.clone.1), kind=kCustom, calls=%fused_computation.15 | custom fusion | bytes 1048578 | tf_op jit(solution)/shard_map/scatter | solution.py:54
  37.3 0.7 reshape.158
  38.0 48.6 %all_to_all.10 = bf16[128,2,2048]{2,1,0:T(2,128)(2,1)S(1)} all-to-all(bf16[128,2,2048]{2,1,0:T(2,128)(2,1)S(1)} %reshape.158), channel_id=1, replica_groups=mesh['dp'=4,'ep'=128] {'ep'}, dimensions={0} | all-to-all | bytes 2097152 | tf_op jit(solution)/shard_map/all_to_all | solution.py:57
  86.6 0.4 reshape.159
  87.0 1.6 fusion.5
  88.7 0.0 copy-done
  88.7 2.6 %convolution_convert_fusion = bf16[256,2048]{1,0:T(8,128)(2,1)S(1)} fusion(bf16[256,2048]{1,0:T(8,128)(2,1)S(1)} %reshape.159, bf16[1,192,2048]{2,1,0:T(8,128)(2,1)S(1)} %copy-done, bf16[1,2,192,2048]{3,2,1,0:T(8,128)(2,1)} %param.8, f32[256,192]{0,1:T(8,128)S(1)} %fusion.5), kind=kOutput, calls=%fused_computation.4 | convolution fusion | flops 403472384 | bytes 3866624 | tf_op jit(solution)/shard_map/dot_general | solution.py:17
  91.2 1.5 reshape.160
  92.8 5.9 %all-to-all-start.1 = ((bf16[128,2,2048]{2,1,0:T(2,128)(2,1)}), bf16[128,2,2048]{2,1,0:T(2,128)(2,1)S(1)}, u32[]{:S(2)}, u32[]{:S(2)}) async-start(bf16[128,2,2048]{2,1,0:T(2,128)(2,1)} %reshape.160), calls=%async_computation.1 | async-start | bytes 2097152 | tf_op jit(solution)/shard_map/all_to_all | solution.py:60
  98.7 0.0 all-reduce.3.cloned.1.call-start
  98.8 0.2 fusion.21
  98.9 0.1 fusion.20
  99.0 31.1 %all-to-all-done.1 = bf16[128,2,2048]{2,1,0:T(2,128)(2,1)S(1)} async-done(((bf16[128,2,2048]{2,1,0:T(2,128)(2,1)}), bf16[128,2,2048]{2,1,0:T(2,128)(2,1)S(1)}, u32[]{:S(2)}, u32[]{:S(2)}) %all-to-all-start.1) | async-done | bytes 1048608 | tf_op jit(solution)/shard_map/all_to_all | solution.py:60
  130.1 0.4 reshape.161
  130.6 0.9 gather_fusion.1
  131.5 1.1 fusion.1
  132.6 0.0 all-reduce.3.cloned.1.call-update
  132.6 1.3 dynamic-slice
  134.5 41.4 %all-reduce.3.cloned.1.call-done = bf16[16,2048]{1,0:T(8,128)(2,1)} async-done(((bf16[16,2048]{1,0:T(8,128)(2,1)}), bf16[16,2048]{1,0:T(8,128)(2,1)}) %all-reduce.3.cloned.1.call-update) | async-done | bytes 65552
  175.9 1.4 dynamic-slice_bitcast_fusion
  (8 shorter events, 0.1 us)
Async XLA Ops:
  6.5 82.1 %copy-start = (bf16[1,192,2048]{2,1,0:T(8,128)(2,1)S(1)}, bf16[1,192,2048]{2,1,0:T(8,128)(2,1)}, u32[]{:S(2)}) copy-start(bf16[1,192,2048]{2,1,0:T(8,128)(2,1)} %param.9) | copy-start | bytes 2359300
  6.5 19.1 %collective-permute-start = (bf16[4,2048]{1,0:T(4,128)(2,1)}, bf16[4,2048]{1,0:T(4,128)(2,1)S(1)}, u32[]{:S(2)}, u32[]{:S(2)}) collective-permute-start(bf16[4,2048]{1,0:T(4,128)(2,1)} %bitcast.40), channel_id=1, source_target_pairs={{0,128},{128,256},{256,384},{384,0},{1,129},{129,257},{257,385},{3... | collective-permute-start | bytes 49160 | tf_op jit(solution)/shard_map/ppermute | solution.py:44
  10.1 18.2 %collective-permute-start.2 = (bf16[4,2048]{1,0:T(4,128)(2,1)}, bf16[4,2048]{1,0:T(4,128)(2,1)S(1)}, u32[]{:S(2)}, u32[]{:S(2)}) collective-permute-start(bf16[4,2048]{1,0:T(4,128)(2,1)} %bitcast.41), channel_id=1, source_target_pairs={{128,0},{256,128},{384,256},{0,384},{129,1},{257,129},{385,257},{1... | collective-permute-start | bytes 49160 | tf_op jit(solution)/shard_map/ppermute | solution.py:46
  25.6 6.8 %collective-permute-start.1 = (bf16[4,2048]{1,0:T(4,128)(2,1)S(1)}, bf16[4,2048]{1,0:T(4,128)(2,1)S(1)}, u32[]{:S(2)}, u32[]{:S(2)}) collective-permute-start(bf16[4,2048]{1,0:T(4,128)(2,1)S(1)} %collective-permute-done), channel_id=1, source_target_pairs={{0,128},{128,256},{256,384},{384,0},{1,129},{129,257},{257,385},{3... | collective-permute-start | bytes 49160 | tf_op jit(solution)/shard_map/ppermute | solution.py:44
  92.8 37.4 %all-to-all-start.1 = ((bf16[128,2,2048]{2,1,0:T(2,128)(2,1)}), bf16[128,2,2048]{2,1,0:T(2,128)(2,1)S(1)}, u32[]{:S(2)}, u32[]{:S(2)}) async-start(bf16[128,2,2048]{2,1,0:T(2,128)(2,1)} %reshape.160), calls=%async_computation.1 | async-start | bytes 2097152 | tf_op jit(solution)/shard_map/all_to_all | solution.py:60
  98.7 77.2 %all-reduce.3.cloned.1.call-start = ((), (), s32[]{:S(2)}) async-start(), calls=%async_computation.2 | async-start | bytes 131072
Sparse Core Ops, SparseCore 0:
  132.7 43.1 all-reduce.2
